TPU v7x, 32 devices: a whole 2x2x4 slice. The times are simulated.
32 devices in a mesh: ctx: 8 (over y, x, core), head: 4 (over z).
Axes of the slice: x: 2, y: 2, z: 4, core: 2. Of those that a mesh axis runs over, the one named last changes fastest.
Arguments:
- q_nope: bfloat16 [512, 8192], P('ctx', 'head'), may hold values from -0.59765625 to 0.59765625
- q_rope: bfloat16 [512, 4096], P('ctx', 'head'), may hold values from -6 to 6
- w_uk: bfloat16 [64, 128, 512], P('head'), may hold values from -0.5 to 0.5
- w_uv: bfloat16 [64, 512, 128], P('head'), may hold values from -0.25 to 0.25
- w_o: bfloat16 [8192, 7168], P('head'), may hold values from -0.0625 to 0.0625
- latent_cache: bfloat16 [576, 8192], P(None, 'ctx'), may hold values from -36 to 36
- group_start: int32 [1], replicated, may hold values from 2048 to 7680
Outputs:
- attention_out: bfloat16 [512, 7168], P('ctx', 'head')
All inputs are finite; a program needn't handle non-finite values.
Results may differ from a plain program's by a relative error of at most 0.02.
Values may be sent and summed in bfloat16 or wider, within the bound.
A program may use at most 128 MiB of HBM per device.

v0:
```python
import functools
import math

import jax
import jax.numpy as jnp
from jax import lax
from jax.experimental import pallas as pl
from jax.experimental.pallas import tpu as pltpu
from jax.sharding import PartitionSpec as P

LATENT = 512
ROPE = 64
NOPE = 128
VDIM = 128
MESH = pl.DeviceIdType.MESH

masked_score = -1e30
floor_score = -1e29


def score_scale():
    return (NOPE + ROPE) ** (-0.5) * (0.1 * math.log(32.0) + 1.0) ** 2


def exponent_scale():
    return score_scale() * math.log2(math.e)


def peer_chip(chip, step, chips):
    if chips & (chips - 1):
        return lax.rem(chip + step, chips) if step >= 0 else chip
    total = 0
    bit = 1
    while bit < chips:
        flip = 1 if step & bit else 0
        total = total + lax.rem(chip // bit + flip, 2) * bit
        bit *= 2
    return total


def kernel(
    devices, heads_axis, tokens, half, slots, columns,
    start_ref, qn_hbm, qr_hbm, uk_hbm, uv_hbm, wo_hbm, cache_hbm, out_ref,
    wo, keys, values, cache, uk, uv, qn, qr, scores, weights, bias,
    hv_send, hv_recv, lse_send, lse_recv, mix, hv, part, parts_sent, down, up,
    loc_sem, wo_sem, cache_sems, q_send, q_recv, hv_send_sem, hv_recv_sem,
    lse_send_sem, lse_recv_sem, down_send, down_recv, up_send, up_recv,
):
    chips = devices // 2
    me = lax.axis_index("ctx")
    row = lax.axis_index("head")
    chip = me // 2
    core = lax.rem(me, 2)
    other = 1 - core
    partner = chip * 2 + other
    wide = half * NOPE
    roped = half * ROPE
    span = 2 * slots
    pair = 2 * tokens
    local = []

    def begin(src, dst, sem):
        copy = pltpu.make_async_copy(src, dst, sem)
        copy.start()
        return copy

    own_cache = begin(cache_hbm, cache.at[core], loc_sem.at[0])
    own_uk = begin(uk_hbm.at[pl.ds(core * half, half)], uk, loc_sem.at[1])
    own_uv = begin(uv_hbm.at[pl.ds(core * half, half)], uv, loc_sem.at[2])

    def half_n(which):
        return qn_hbm.at[:, pl.ds(pl.multiple_of(which * wide, 128), wide)]

    def half_r(which):
        return qr_hbm.at[:, pl.ds(pl.multiple_of(which * roped, 128), roped)]

    own_qn = begin(half_n(core), qn.at[me], loc_sem.at[3])
    own_qr = begin(half_r(core), qr.at[me], loc_sem.at[4])

    barrier = pltpu.get_barrier_semaphore()
    for step in range(1, devices):
        pl.semaphore_signal(
            barrier, inc=1, device_id={"ctx": lax.rem(me + step, devices)}, device_id_type=MESH
        )

    @pl.when(row > 0)
    def _():
        pl.semaphore_signal(barrier, inc=1, device_id={"head": row - 1}, device_id_type=MESH)

    @pl.when(row < heads_axis - 1)
    def _():
        pl.semaphore_signal(barrier, inc=1, device_id={"head": row + 1}, device_id_type=MESH)

    below = (row + heads_axis - 1) // heads_axis
    above = (2 * heads_axis - 2 - row) // heads_axis
    pl.semaphore_wait(barrier, devices - 1 + below + above)

    def remote(src, dst, send, recv, target):
        return pltpu.make_async_remote_copy(
            src_ref=src, dst_ref=dst, send_sem=send, recv_sem=recv,
            device_id=target, device_id_type=MESH,
        )

    cache_out = remote(
        cache_hbm, cache.at[core], cache_sems.at[0], cache_sems.at[1], {"ctx": partner}
    )
    cache_out.start()
    sent = []

    def send_q(step):
        target_chip = peer_chip(chip, step, chips)
        for which in range(2):
            index = step * 2 + which
            target = {"ctx": target_chip * 2 + which}
            mine = step * 2 + core
            for copy in (
                remote(half_n(which), qn.at[me], q_send.at[index, 0], q_recv.at[mine, 0], target),
                remote(half_r(which), qr.at[me], q_send.at[index, 1], q_recv.at[mine, 1], target),
            ):
                copy.start()
                sent.append(copy)

    for step in range(1, min(3, chips)):
        send_q(step)
    for copy in (
        remote(half_n(other), qn.at[me], q_send.at[0, 0], q_recv.at[core, 0], {"ctx": partner}),
        remote(half_r(other), qr.at[me], q_send.at[0, 1], q_recv.at[core, 1], {"ctx": partner}),
    ):
        copy.start()
        sent.append(copy)
    weight_copies = []
    for dest in range(heads_axis):
        weight_copies.append(
            begin(wo_hbm.at[:, dest * columns:(dest + 1) * columns], wo.at[dest], wo_sem.at[dest])
        )

    scale = exponent_scale()
    own_uk.wait()
    own_uv.wait()
    chunk = 256

    def expand(place):
        uk_rows = uk[...].reshape(half * NOPE, LATENT)
        value_rows = [uv[h].T for h in range(half)]
        value_rows = jnp.concatenate(value_rows, axis=0)

        def body(i, carry):
            here = pl.multiple_of(i * chunk, chunk)
            block = cache[place, :, pl.ds(here, chunk)]
            turned = block.T
            spot = pl.ds(pl.multiple_of(place * slots + here, chunk), chunk)
            nope = lax.dot_general(
                turned[:, :LATENT], uk_rows, (((1,), (1,)), ((), ())),
                preferred_element_type=jnp.float32,
            )
            nope = (nope * scale).astype(jnp.bfloat16)
            rope = (turned[:, LATENT:].astype(jnp.float32) * scale).astype(jnp.bfloat16)
            blank = jnp.zeros_like(rope)
            even = jnp.concatenate([rope, blank], axis=1)
            odd = jnp.concatenate([blank, rope], axis=1)
            for h in range(half):
                keys[h, spot, :NOPE] = nope[:, h * NOPE:(h + 1) * NOPE]
                keys[h, spot, NOPE:] = odd if h % 2 else even
            values[:, spot] = jnp.dot(
                value_rows, block[:LATENT], preferred_element_type=jnp.float32
            ).astype(jnp.bfloat16)
            return carry

        lax.fori_loop(0, slots // chunk, body, 0)

    own_cache.wait()
    expand(core)
    remote(
        cache_hbm, cache.at[other], cache_sems.at[0], cache_sems.at[1], {"ctx": partner}
    ).wait_recv()
    expand(other)
    for step in range(3, chips):
        send_q(step)

    order = list(range(1, chips)) + [0]
    lse_send[...] = jnp.zeros_like(lse_send)
    group_start = start_ref[0]
    block_rows = min(512, span)

    for phase in range(chips // 2):
        both = order[2 * phase:2 * phase + 2]
        sources = []
        for step in both:
            source_chip = peer_chip(chip, step, chips)
            for c in range(2):
                sources.append(source_chip * 2 + c)
            if step == 0:
                own_qn.wait()
                own_qr.wait()
                remote(half_n(core), qn.at[partner], q_send.at[0, 0], q_recv.at[other, 0], {"ctx": partner}).wait_recv()
                remote(half_r(core), qr.at[partner], q_send.at[0, 1], q_recv.at[other, 1], {"ctx": partner}).wait_recv()
            else:
                for c in range(2):
                    src = source_chip * 2 + c
                    index = step * 2 + c
                    remote(half_n(core), qn.at[src], q_send.at[index, 0], q_recv.at[index, 0], {"ctx": src}).wait_recv()
                    remote(half_r(core), qr.at[src], q_send.at[index, 1], q_recv.at[index, 1], {"ctx": src}).wait_recv()
        lanes = lax.broadcasted_iota(jnp.int32, (1, 2 * pair), 1)
        token = jnp.zeros((1, 2 * pair), jnp.int32)
        for i, src in enumerate(sources):
            token = jnp.where(lanes // tokens == i, src * tokens + lanes - i * tokens, token)
        position = token + group_start

        def fill(i, carry):
            here = pl.multiple_of(i * chunk, chunk)
            slot = lax.broadcasted_iota(jnp.int32, (chunk, 2 * pair), 0) + (chip * span + here)
            bias[pl.ds(here, chunk), :] = jnp.where(slot <= position, 0.0, masked_score)
            return carry

        lax.fori_loop(0, span // chunk, fill, 0)

        def head_pair(j, carry):
            for parity in range(2):
                h = j * 2 + parity
                n_cols = pl.ds(pl.multiple_of(h * NOPE, NOPE), NOPE)
                r_cols = pl.ds(pl.multiple_of(j * NOPE, NOPE), NOPE)
                query = jnp.concatenate(
                    [
                        jnp.concatenate([qn[src, :, n_cols], qr[src, :, r_cols]], axis=1)
                        for src in sources
                    ],
                    axis=0,
                )
                best = jnp.full((1, 2 * pair), floor_score, jnp.float32)
                for b in range(span // block_rows):
                    rows = slice(b * block_rows, (b + 1) * block_rows)
                    s = lax.dot_general(
                        keys[h, rows, :], query, (((1,), (1,)), ((), ())),
                        preferred_element_type=jnp.float32,
                    ) + bias[rows, :]
                    scores[parity, rows, :] = s
                    best = jnp.maximum(best, jnp.max(s, axis=0, keepdims=True))
                total = jnp.zeros((1, 2 * pair), jnp.float32)
                for b in range(span // block_rows):
                    rows = slice(b * block_rows, (b + 1) * block_rows)
                    p = jnp.exp2(scores[parity, rows, :] - best)
                    total = total + jnp.sum(p, axis=0, keepdims=True)
                    weights[parity, rows, :] = p.astype(jnp.bfloat16)
                v_rows = pl.ds(pl.multiple_of(h * VDIM, VDIM), VDIM)
                o = jnp.dot(values[v_rows, :], weights[parity], preferred_element_type=jnp.float32)
                safe = jnp.maximum(total, 1e-30)
                o = (o / safe).T.astype(jnp.bfloat16)
                lse = best + jnp.log2(safe)
                for i in range(2):
                    hv_send[2 * phase + i, :, n_cols] = o[i * pair:(i + 1) * pair]
                    lse_send[2 * phase + i, pl.ds(h, 1), :] = lse[:, i * pair:(i + 1) * pair]
            return carry

        lax.fori_loop(0, half // 2, head_pair, 0)

        for i, step in enumerate(both):
            slot = 2 * phase + i
            target_chip = peer_chip(chip, step, chips)
            if step == 0:
                data = hv_send.at[slot, pl.ds(pl.multiple_of(other * tokens, tokens), tokens)]
                kept = hv_send.at[slot, pl.ds(pl.multiple_of(core * tokens, tokens), tokens)]
                local.append(begin(kept, hv_recv.at[chip, core], loc_sem.at[5]))
                local.append(begin(lse_send.at[slot], lse_recv.at[chip, core], loc_sem.at[6]))
                out = [
                    remote(data, hv_recv.at[chip, core], hv_send_sem.at[0], hv_recv_sem.at[core], {"ctx": partner}),
                    remote(lse_send.at[slot], lse_recv.at[chip, core], lse_send_sem.at[0], lse_recv_sem.at[core], {"ctx": partner}),
                ]
            else:
                out = []
                for c in range(2):
                    data = hv_send.at[slot, c * tokens:(c + 1) * tokens]
                    target = {"ctx": target_chip * 2 + c}
                    out.append(remote(data, hv_recv.at[chip, core], hv_send_sem.at[step * 2 + c], hv_recv_sem.at[step * 2 + core], target))
                    out.append(remote(lse_send.at[slot], lse_recv.at[chip, core], lse_send_sem.at[step * 2 + c], lse_recv_sem.at[step * 2 + core], target))
            for copy in out:
                copy.start()
                sent.append(copy)

    for copy in local:
        copy.wait()
    for step in order:
        source_chip = peer_chip(chip, step, chips)
        for c in [other] if step == 0 else [0, 1]:
            index = step * 2 + c
            src = {"ctx": source_chip * 2 + c}
            remote(hv_send.at[0, :tokens], hv_recv.at[source_chip, c], hv_send_sem.at[0], hv_recv_sem.at[index], src).wait_recv()
            remote(lse_send.at[0], lse_recv.at[source_chip, c], lse_send_sem.at[0], lse_recv_sem.at[index], src).wait_recv()

    for c in range(2):
        found = [lse_recv[i, c] for i in range(chips)]
        top = functools.reduce(jnp.maximum, found)
        shares = [jnp.exp2(f - top) for f in found]
        whole = functools.reduce(jnp.add, shares)
        for i in range(chips):
            mix[i] = (shares[i] / whole).T
        mine = pl.ds(pl.multiple_of(core * tokens, tokens), tokens)
        share = [mix[i, mine, :] for i in range(chips)]
        for h in range(half):
            cols = slice(h * VDIM, (h + 1) * VDIM)
            total = jnp.zeros((tokens, VDIM), jnp.float32)
            for i in range(chips):
                total = total + hv_recv[i, c, :, cols].astype(jnp.float32) * share[i][:, h:h + 1]
            hv[:, c * half * VDIM + h * VDIM:c * half * VDIM + (h + 1) * VDIM] = total.astype(jnp.bfloat16)

    for copy in weight_copies:
        copy.wait()
    piece = math.gcd(columns, 896)

    def project(dest):
        for b in range(columns // piece):
            cols = slice(b * piece, (b + 1) * piece)
            part[:, cols] = jnp.dot(hv[...], wo[dest, :, cols], preferred_element_type=jnp.float32)

    last = heads_axis - 1

    def down_copy(dest):
        return remote(parts_sent.at[dest], down.at[dest], down_send.at[dest], down_recv.at[dest], {"head": row + 1})

    def up_copy(dest):
        return remote(parts_sent.at[dest], up.at[dest], up_send.at[dest], up_recv.at[dest], {"head": row - 1})

    def down_wait(dest):
        remote(parts_sent.at[dest], down.at[dest], down_send.at[dest], down_recv.at[dest], {"head": row - 1}).wait_recv()

    def up_wait(dest):
        remote(parts_sent.at[dest], up.at[dest], up_send.at[dest], up_recv.at[dest], {"head": row + 1}).wait_recv()

    at_end = row // last

    def make_part(i, carry):
        dest = last - i + at_end * (2 * i - last)
        project(dest)
        parts_sent[dest] = part[...].astype(jnp.bfloat16)

        @pl.when((row == 0) & (dest > 0))
        def _():
            down_copy(dest).start()

        @pl.when((row == last) & (dest < last))
        def _():
            up_copy(dest).start()

        return carry

    lax.fori_loop(0, heads_axis, make_part, 0)

    upper = (2 * row) // heads_axis
    for i in range(heads_axis):
        turn = last - i // 2 if i % 2 == 0 else i // 2
        dest = turn + upper * (last - 2 * turn)

        @pl.when((row < dest) & (row > 0))
        def _():
            down_wait(dest)
            parts_sent[dest] = parts_sent[dest] + down[dest]
            down_copy(dest).start()

        @pl.when((row > dest) & (row < last))
        def _():
            up_wait(dest)
            parts_sent[dest] = parts_sent[dest] + up[dest]
            up_copy(dest).start()

    part[...] = parts_sent[row].astype(jnp.float32)

    @pl.when(row > 0)
    def _():
        down_wait(row)
        part[...] = part[...] + down[row].astype(jnp.float32)

    @pl.when(row < last)
    def _():
        up_wait(row)
        part[...] = part[...] + up[row].astype(jnp.float32)

    out_ref[...] = part[...].astype(jnp.bfloat16)

    for dest in range(heads_axis):
        @pl.when(row < dest)
        def _():
            down_copy(dest).wait_send()

        @pl.when(row > dest)
        def _():
            up_copy(dest).wait_send()

    cache_out.wait_send()
    for copy in sent:
        copy.wait_send()


def on_device(devices, heads_axis, q_nope, q_rope, w_uk, w_uv, w_o, latent_cache, group_start):
    tokens = q_nope.shape[0]
    half = w_uk.shape[0] // 2
    slots = latent_cache.shape[1]
    width = latent_cache.shape[0]
    columns = w_o.shape[1] // heads_axis
    chips = devices // 2
    pair = 2 * tokens
    span = 2 * slots
    stat_rows = max(8, half)
    bf16, f32 = jnp.bfloat16, jnp.float32
    dma = pltpu.SemaphoreType.DMA
    any_space = pl.BlockSpec(memory_space=pl.ANY)
    return pl.pallas_call(
        functools.partial(kernel, devices, heads_axis, tokens, half, slots, columns),
        out_shape=jax.ShapeDtypeStruct((tokens, columns), bf16),
        in_specs=[pl.BlockSpec(memory_space=pltpu.SMEM)] + [any_space] * 6,
        out_specs=pl.BlockSpec(memory_space=pltpu.VMEM),
        scratch_shapes=[
            pltpu.VMEM((heads_axis, w_o.shape[0], columns), bf16),
            pltpu.VMEM((half, span, 2 * NOPE), bf16),
            pltpu.VMEM((half * VDIM, span), bf16),
            pltpu.VMEM((2, width, slots), bf16),
            pltpu.VMEM((half, NOPE, LATENT), bf16),
            pltpu.VMEM((half, LATENT, VDIM), bf16),
            pltpu.VMEM((devices, tokens, half * NOPE), bf16),
            pltpu.VMEM((devices, tokens, half * ROPE), bf16),
            pltpu.VMEM((2, span, 2 * pair), f32),
            pltpu.VMEM((2, span, 2 * pair), bf16),
            pltpu.VMEM((span, 2 * pair), f32),
            pltpu.VMEM((chips, pair, half * VDIM), bf16),
            pltpu.VMEM((chips, 2, tokens, half * VDIM), bf16),
            pltpu.VMEM((chips, stat_rows, pair), f32),
            pltpu.VMEM((chips, 2, stat_rows, pair), f32),
            pltpu.VMEM((chips, pair, stat_rows), f32),
            pltpu.VMEM((tokens, 2 * half * VDIM), bf16),
            pltpu.VMEM((tokens, columns), f32),
            pltpu.VMEM((heads_axis, tokens, columns), bf16),
            pltpu.VMEM((heads_axis, tokens, columns), bf16),
            pltpu.VMEM((heads_axis, tokens, columns), bf16),
            dma((7,)),
            dma((heads_axis,)),
            dma((2,)),
            dma((devices, 2)),
            dma((devices, 2)),
            dma((devices,)),
            dma((devices,)),
            dma((devices,)),
            dma((devices,)),
            dma((heads_axis,)),
            dma((heads_axis,)),
            dma((heads_axis,)),
            dma((heads_axis,)),
        ],
        compiler_params=pltpu.CompilerParams(
            collective_id=0, has_side_effects=True, vmem_limit_bytes=67043328
        ),
    )(group_start, q_nope, q_rope, w_uk, w_uv, w_o, latent_cache)


def solution(mesh):
    placed = (
        P("ctx", "head"),
        P("ctx", "head"),
        P("head", None, None),
        P("head", None, None),
        P("head", None),
        P(None, "ctx"),
        P(),
    )
    return jax.shard_map(
        functools.partial(on_device, mesh.shape["ctx"], mesh.shape["head"]),
        mesh=mesh, in_specs=placed, out_specs=P("ctx", "head"), check_vma=False,
    )
```

profile of v0, /device:TPU:6, one launch (start us, length us, event | category | flops | bytes accessed | tf_op | source)
XLA Modules:
  0.0 71.3 jit_solution(171515280619865720)
XLA Ops:
  0.7 69.0 %shard_map.73 = bf16[64,1792]{1,0:T(8,128)(2,1)} custom-call(s32[1]{0:T(128)S(6)} %copy.9.start_ref, bf16[64,2048]{1,0:T(8,128)(2,1)} %qn_hbm.1, bf16[64,1024]{1,0:T(8,128)(2,1)} %qr_hbm.1, bf16[16,128,512]{2,1,0:T(8,128)(2,1)} %uk_hbm.1, bf16[16,512,128]{2,1,0:T(8,128)(2,1)} %uv_hbm.1, bf16[2048,7168]{1,0:T(8,128)(2,1)} %wo_hbm.1, bf16[576,1024]{1,0:T(8,128)(2,1)} %cache_hbm.1), custom_call_target="tpu_custom_call" | custom-call | tf_op jit(solution)/shard_map/pallas_call | solution.py:405
  69.6 1.6 %copy.10 = bf16[64,1792]{1,0:T(8,128)(2,1)} copy(bf16[64,1792]{1,0:T(8,128)(2,1)} %shard_map.73) | data formatting | bytes 458752
where the time goes:
time: 71.4 us; the launch traced here: 71.3 us
  Pallas kernels  69 us (97%)
  local copies, waits for them, and re-layouts  1.64 us (2%)
    pallas_call x1, Pallas kernels, on_device(): pl.pallas_call(functools.partial(kernel, devices, heads_axis, tokens, hal...  69 us
    unnamed x1, local copies, waits for them, and re-layouts  1.64 us

commit v1 on v0

v1 whole, which is shorter than its diff:
```python
import functools
import math

import jax
import jax.numpy as jnp
from jax import lax
from jax.experimental import pallas as pl
from jax.experimental.pallas import tpu as pltpu
from jax.sharding import PartitionSpec as P

LATENT = 512
ROPE = 64
NOPE = 128
VDIM = 128
MESH = pl.DeviceIdType.MESH

masked_score = -1e30
floor_score = -1e29


def score_scale():
    return (NOPE + ROPE) ** (-0.5) * (0.1 * math.log(32.0) + 1.0) ** 2


def exponent_scale():
    return score_scale() * math.log2(math.e)


def peer_chip(chip, step, chips):
    assert chips & (chips - 1) == 0
    total = 0
    bit = 1
    while bit < chips:
        flip = 1 if step & bit else 0
        total = total + lax.rem(chip // bit + flip, 2) * bit
        bit *= 2
    return total


def kernel(
    devices, heads_axis, tokens, half, slots, columns,
    start_ref, qn_hbm, qr_hbm, uk_hbm, uv_hbm, wo_hbm, cache_hbm, out_ref,
    wo, keys, values, cache, uk, uv, qn, qr, scores, weights, bias,
    hv_send, hv_recv, lse_send, lse_recv, mix, hv, part, parts_sent, down, up,
    loc_sem, wo_sem, cache_sems, q_send, q_recv, hv_send_sem, hv_recv_sem,
    lse_send_sem, lse_recv_sem, down_send, down_recv, up_send, up_recv,
):
    chips = devices // 2
    me = lax.axis_index("ctx")
    row = lax.axis_index("head")
    chip = me // 2
    core = lax.rem(me, 2)
    other = 1 - core
    partner = chip * 2 + other
    wide = half * NOPE
    roped = half * ROPE
    span = 2 * slots
    part_rows = tokens // 2
    pair = 2 * part_rows
    lanes_total = devices * part_rows
    local = []

    def begin(src, dst, sem):
        copy = pltpu.make_async_copy(src, dst, sem)
        copy.start()
        return copy

    own_cache = begin(cache_hbm, cache.at[core], loc_sem.at[0])
    own_uk = begin(uk_hbm.at[pl.ds(core * half, half)], uk, loc_sem.at[1])
    own_uv = begin(uv_hbm.at[pl.ds(core * half, half)], uv, loc_sem.at[2])

    def rows_of(phase):
        return pl.ds(phase * part_rows, part_rows)

    def half_n(which, phase):
        return qn_hbm.at[rows_of(phase), pl.ds(pl.multiple_of(which * wide, 128), wide)]

    def half_r(which, phase):
        return qr_hbm.at[rows_of(phase), pl.ds(pl.multiple_of(which * roped, 128), roped)]

    own_q = []
    for phase in range(2):
        own_q.append(begin(half_n(core, phase), qn.at[me, rows_of(phase)], loc_sem.at[3 + 2 * phase]))
        own_q.append(begin(half_r(core, phase), qr.at[me, rows_of(phase)], loc_sem.at[4 + 2 * phase]))

    barrier = pltpu.get_barrier_semaphore()
    for step in range(1, devices):
        pl.semaphore_signal(
            barrier, inc=1, device_id={"ctx": lax.rem(me + step, devices)}, device_id_type=MESH
        )

    @pl.when(row > 0)
    def _():
        pl.semaphore_signal(barrier, inc=1, device_id={"head": row - 1}, device_id_type=MESH)

    @pl.when(row < heads_axis - 1)
    def _():
        pl.semaphore_signal(barrier, inc=1, device_id={"head": row + 1}, device_id_type=MESH)

    below = (row + heads_axis - 1) // heads_axis
    above = (2 * heads_axis - 2 - row) // heads_axis
    pl.semaphore_wait(barrier, devices - 1 + below + above)

    def remote(src, dst, send, recv, target):
        return pltpu.make_async_remote_copy(
            src_ref=src, dst_ref=dst, send_sem=send, recv_sem=recv,
            device_id=target, device_id_type=MESH,
        )

    cache_out = remote(
        cache_hbm, cache.at[core], cache_sems.at[0], cache_sems.at[1], {"ctx": partner}
    )
    cache_out.start()
    sent = []

    def q_copies(phase, source, which, target, index, mine):
        rows = rows_of(phase)
        return (
            remote(half_n(which, phase), qn.at[source, rows], q_send.at[phase, index, 0], q_recv.at[phase, mine, 0], {"ctx": target}),
            remote(half_r(which, phase), qr.at[source, rows], q_send.at[phase, index, 1], q_recv.at[phase, mine, 1], {"ctx": target}),
        )

    def send_q(phase):
        for step in range(1, chips):
            target_chip = peer_chip(chip, step, chips)
            for which in range(2):
                for copy in q_copies(phase, me, which, target_chip * 2 + which, step * 2 + which, step * 2 + core):
                    copy.start()
                    sent.append(copy)
        for copy in q_copies(phase, me, other, partner, 0, core):
            copy.start()
            sent.append(copy)

    send_q(0)
    weight_copies = []
    for dest in range(heads_axis):
        weight_copies.append(
            begin(wo_hbm.at[:, dest * columns:(dest + 1) * columns], wo.at[dest], wo_sem.at[dest])
        )

    scale = exponent_scale()
    own_uk.wait()
    own_uv.wait()
    chunk = 256

    def expand(place):
        uk_rows = uk[...].reshape(half * NOPE, LATENT)
        value_rows = [uv[h].T for h in range(half)]
        value_rows = jnp.concatenate(value_rows, axis=0)

        def body(i, carry):
            here = pl.multiple_of(i * chunk, chunk)
            block = cache[place, :, pl.ds(here, chunk)]
            turned = block.T
            spot = pl.ds(pl.multiple_of(place * slots + here, chunk), chunk)
            nope = lax.dot_general(
                turned[:, :LATENT], uk_rows, (((1,), (1,)), ((), ())),
                preferred_element_type=jnp.float32,
            )
            nope = (nope * scale).astype(jnp.bfloat16)
            rope = (turned[:, LATENT:].astype(jnp.float32) * scale).astype(jnp.bfloat16)
            blank = jnp.zeros_like(rope)
            even = jnp.concatenate([rope, blank], axis=1)
            odd = jnp.concatenate([blank, rope], axis=1)
            for h in range(half):
                keys[h, spot, :NOPE] = nope[:, h * NOPE:(h + 1) * NOPE]
                keys[h, spot, NOPE:] = odd if h % 2 else even
            values[:, spot] = jnp.dot(
                value_rows, block[:LATENT], preferred_element_type=jnp.float32
            ).astype(jnp.bfloat16)
            return carry

        lax.fori_loop(0, slots // chunk, body, 0)

    own_cache.wait()
    expand(core)
    send_q(1)
    remote(
        cache_hbm, cache.at[other], cache_sems.at[0], cache_sems.at[1], {"ctx": partner}
    ).wait_recv()
    expand(other)

    order = list(range(1, chips)) + [0]
    lse_send[...] = jnp.zeros_like(lse_send)
    group_start = start_ref[0]
    block_rows = min(512, span)

    for phase in range(2):
        sources = []
        for step in order:
            source_chip = peer_chip(chip, step, chips)
            for c in range(2):
                sources.append(source_chip * 2 + c)
            if step == 0:
                own_q[2 * phase].wait()
                own_q[2 * phase + 1].wait()
                for copy in q_copies(phase, partner, core, partner, 0, other):
                    copy.wait_recv()
            else:
                for c in range(2):
                    src = source_chip * 2 + c
                    for copy in q_copies(phase, src, core, src, step * 2 + c, step * 2 + c):
                        copy.wait_recv()
        lanes = lax.broadcasted_iota(jnp.int32, (1, lanes_total), 1)
        token = jnp.zeros((1, lanes_total), jnp.int32)
        for i, src in enumerate(sources):
            token = jnp.where(
                lanes // part_rows == i,
                src * tokens + phase * part_rows + lanes - i * part_rows, token,
            )
        position = token + group_start

        def fill(i, carry):
            here = pl.multiple_of(i * chunk, chunk)
            slot = lax.broadcasted_iota(jnp.int32, (chunk, lanes_total), 0) + (chip * span + here)
            bias[pl.ds(here, chunk), :] = jnp.where(slot <= position, 0.0, masked_score)
            return carry

        lax.fori_loop(0, span // chunk, fill, 0)

        token_rows = slice(phase * part_rows, (phase + 1) * part_rows)

        def head_pair(j, carry):
            for parity in range(2):
                h = j * 2 + parity
                n_cols = pl.ds(pl.multiple_of(h * NOPE, NOPE), NOPE)
                r_cols = pl.ds(pl.multiple_of(j * NOPE, NOPE), NOPE)
                query = jnp.concatenate(
                    [
                        jnp.concatenate([qn[src, token_rows, n_cols], qr[src, token_rows, r_cols]], axis=1)
                        for src in sources
                    ],
                    axis=0,
                )
                best = jnp.full((1, lanes_total), floor_score, jnp.float32)
                for b in range(span // block_rows):
                    rows = slice(b * block_rows, (b + 1) * block_rows)
                    s = lax.dot_general(
                        keys[h, rows, :], query, (((1,), (1,)), ((), ())),
                        preferred_element_type=jnp.float32,
                    ) + bias[rows, :]
                    scores[parity, rows, :] = s
                    best = jnp.maximum(best, jnp.max(s, axis=0, keepdims=True))
                total = jnp.zeros((1, lanes_total), jnp.float32)
                for b in range(span // block_rows):
                    rows = slice(b * block_rows, (b + 1) * block_rows)
                    p = jnp.exp2(scores[parity, rows, :] - best)
                    total = total + jnp.sum(p, axis=0, keepdims=True)
                    weights[parity, rows, :] = p.astype(jnp.bfloat16)
                v_rows = pl.ds(pl.multiple_of(h * VDIM, VDIM), VDIM)
                o = jnp.dot(values[v_rows, :], weights[parity], preferred_element_type=jnp.float32)
                safe = jnp.maximum(total, 1e-30)
                o = (o / safe).T.astype(jnp.bfloat16)
                lse = best + jnp.log2(safe)
                for i in range(chips):
                    hv_send[phase, i, :, n_cols] = o[i * pair:(i + 1) * pair]
                for i in range(chips // 2):
                    lse_send[phase, i, pl.ds(h, 1), :] = lse[:, 2 * i * pair:2 * (i + 1) * pair]
            return carry

        lax.fori_loop(0, half // 2, head_pair, 0)

        for i, step in enumerate(order):
            target_chip = peer_chip(chip, step, chips)
            stats = lse_send.at[phase, i // 2]
            for c in range(2):
                if step == 0 and c == 1:
                    continue
                index = step * 2 + c
                if step == 0:
                    data = hv_send.at[phase, i, pl.ds(pl.multiple_of(other * part_rows, part_rows), part_rows)]
                    kept = hv_send.at[phase, i, pl.ds(pl.multiple_of(core * part_rows, part_rows), part_rows)]
                    local.append(begin(kept, hv_recv.at[phase, i, core], loc_sem.at[7 + 2 * phase]))
                    local.append(begin(stats, lse_recv.at[phase, i, core], loc_sem.at[8 + 2 * phase]))
                    target = {"ctx": partner}
                else:
                    data = hv_send.at[phase, i, c * part_rows:(c + 1) * part_rows]
                    target = {"ctx": target_chip * 2 + c}
                mine = step * 2 + core
                for copy in (
                    remote(data, hv_recv.at[phase, i, core], hv_send_sem.at[phase, index], hv_recv_sem.at[phase, mine], target),
                    remote(stats, lse_recv.at[phase, i, core], lse_send_sem.at[phase, index], lse_recv_sem.at[phase, mine], target),
                ):
                    copy.start()
                    sent.append(copy)

    def combine(phase):
        local[2 * phase].wait()
        local[2 * phase + 1].wait()
        for i, step in enumerate(order):
            source_chip = peer_chip(chip, step, chips)
            for c in [other] if step == 0 else [0, 1]:
                index = step * 2 + c
                src = {"ctx": source_chip * 2 + c}
                remote(hv_send.at[phase, 0, :part_rows], hv_recv.at[phase, i, c], hv_send_sem.at[phase, 0], hv_recv_sem.at[phase, index], src).wait_recv()
                remote(lse_send.at[phase, 0], lse_recv.at[phase, i, c], lse_send_sem.at[phase, 0], lse_recv_sem.at[phase, index], src).wait_recv()
        for c in range(2):
            found = []
            for i in range(chips):
                mix[i] = lse_recv[phase, i, c].T
                first = pl.multiple_of((i % 2) * pair + core * part_rows, part_rows)
                found.append(mix[i, pl.ds(first, part_rows), :])
            top = functools.reduce(jnp.maximum, found)
            shares = [jnp.exp2(f - top) for f in found]
            whole = functools.reduce(jnp.add, shares)
            share = [f / whole for f in shares]
            for h in range(half):
                cols = slice(h * VDIM, (h + 1) * VDIM)
                total = jnp.zeros((part_rows, VDIM), jnp.float32)
                for i in range(chips):
                    total = total + hv_recv[phase, i, c, :, cols].astype(jnp.float32) * share[i][:, h:h + 1]
                first = (c * half + h) * VDIM
                hv[:, first:first + VDIM] = total.astype(jnp.bfloat16)

    piece = math.gcd(columns, 896)

    def project(dest):
        for b in range(columns // piece):
            cols = slice(b * piece, (b + 1) * piece)
            part[:, cols] = jnp.dot(hv[...], wo[dest, :, cols], preferred_element_type=jnp.float32)

    last = heads_axis - 1

    def chain(phase, dest, buffer, sends, recvs, target):
        return remote(parts_sent.at[phase, dest], buffer.at[phase, dest], sends.at[phase, dest], recvs.at[phase, dest], {"head": target})

    def down_copy(phase, dest):
        return chain(phase, dest, down, down_send, down_recv, row + 1)

    def up_copy(phase, dest):
        return chain(phase, dest, up, up_send, up_recv, row - 1)

    def down_wait(phase, dest):
        chain(phase, dest, down, down_send, down_recv, row - 1).wait_recv()

    def up_wait(phase, dest):
        chain(phase, dest, up, up_send, up_recv, row + 1).wait_recv()

    at_end = row // last
    upper = (2 * row) // heads_axis

    for phase in range(2):
        combine(phase)
        if phase == 0:
            for copy in weight_copies:
                copy.wait()

        def make_part(i, carry):
            dest = last - i + at_end * (2 * i - last)
            project(dest)
            parts_sent[phase, dest] = part[...].astype(jnp.bfloat16)

            @pl.when((row == 0) & (dest > 0))
            def _():
                down_copy(phase, dest).start()

            @pl.when((row == last) & (dest < last))
            def _():
                up_copy(phase, dest).start()

            return carry

        lax.fori_loop(0, heads_axis, make_part, 0)

        for i in range(heads_axis):
            turn = last - i // 2 if i % 2 == 0 else i // 2
            dest = turn + upper * (last - 2 * turn)

            @pl.when((row < dest) & (row > 0))
            def _():
                down_wait(phase, dest)
                parts_sent[phase, dest] = parts_sent[phase, dest] + down[phase, dest]
                down_copy(phase, dest).start()

            @pl.when((row > dest) & (row < last))
            def _():
                up_wait(phase, dest)
                parts_sent[phase, dest] = parts_sent[phase, dest] + up[phase, dest]
                up_copy(phase, dest).start()

    for phase in range(2):
        part[...] = parts_sent[phase, row].astype(jnp.float32)

        @pl.when(row > 0)
        def _():
            down_wait(phase, row)
            part[...] = part[...] + down[phase, row].astype(jnp.float32)

        @pl.when(row < last)
        def _():
            up_wait(phase, row)
            part[...] = part[...] + up[phase, row].astype(jnp.float32)

        out_ref[phase * part_rows:(phase + 1) * part_rows, :] = part[...].astype(jnp.bfloat16)

    for phase in range(2):
        for dest in range(heads_axis):
            @pl.when(row < dest)
            def _():
                down_copy(phase, dest).wait_send()

            @pl.when(row > dest)
            def _():
                up_copy(phase, dest).wait_send()

    cache_out.wait_send()
    for copy in sent:
        copy.wait_send()


def on_device(devices, heads_axis, q_nope, q_rope, w_uk, w_uv, w_o, latent_cache, group_start):
    tokens = q_nope.shape[0]
    half = w_uk.shape[0] // 2
    slots = latent_cache.shape[1]
    width = latent_cache.shape[0]
    columns = w_o.shape[1] // heads_axis
    chips = devices // 2
    part_rows = tokens // 2
    pair = 2 * part_rows
    lanes_total = devices * part_rows
    span = 2 * slots
    stat_rows = max(8, half)
    bf16, f32 = jnp.bfloat16, jnp.float32
    dma = pltpu.SemaphoreType.DMA
    any_space = pl.BlockSpec(memory_space=pl.ANY)
    return pl.pallas_call(
        functools.partial(kernel, devices, heads_axis, tokens, half, slots, columns),
        out_shape=jax.ShapeDtypeStruct((tokens, columns), bf16),
        in_specs=[pl.BlockSpec(memory_space=pltpu.SMEM)] + [any_space] * 6,
        out_specs=pl.BlockSpec(memory_space=pltpu.VMEM),
        scratch_shapes=[
            pltpu.VMEM((heads_axis, w_o.shape[0], columns), bf16),
            pltpu.VMEM((half, span, 2 * NOPE), bf16),
            pltpu.VMEM((half * VDIM, span), bf16),
            pltpu.VMEM((2, width, slots), bf16),
            pltpu.VMEM((half, NOPE, LATENT), bf16),
            pltpu.VMEM((half, LATENT, VDIM), bf16),
            pltpu.VMEM((devices, tokens, half * NOPE), bf16),
            pltpu.VMEM((devices, tokens, half * ROPE), bf16),
            pltpu.VMEM((2, span, lanes_total), f32),
            pltpu.VMEM((2, span, lanes_total), bf16),
            pltpu.VMEM((span, lanes_total), f32),
            pltpu.VMEM((2, chips, pair, half * VDIM), bf16),
            pltpu.VMEM((2, chips, 2, part_rows, half * VDIM), bf16),
            pltpu.VMEM((2, chips // 2, stat_rows, 2 * pair), f32),
            pltpu.VMEM((2, chips, 2, stat_rows, 2 * pair), f32),
            pltpu.VMEM((chips, 2 * pair, stat_rows), f32),
            pltpu.VMEM((part_rows, 2 * half * VDIM), bf16),
            pltpu.VMEM((part_rows, columns), f32),
            pltpu.VMEM((2, heads_axis, part_rows, columns), bf16),
            pltpu.VMEM((2, heads_axis, part_rows, columns), bf16),
            pltpu.VMEM((2, heads_axis, part_rows, columns), bf16),
            dma((11,)),
            dma((heads_axis,)),
            dma((2,)),
            dma((2, devices, 2)),
            dma((2, devices, 2)),
            dma((2, devices)),
            dma((2, devices)),
            dma((2, devices)),
            dma((2, devices)),
            dma((2, heads_axis)),
            dma((2, heads_axis)),
            dma((2, heads_axis)),
            dma((2, heads_axis)),
        ],
        compiler_params=pltpu.CompilerParams(
            collective_id=0, has_side_effects=True, vmem_limit_bytes=67043328
        ),
    )(group_start, q_nope, q_rope, w_uk, w_uv, w_o, latent_cache)


def solution(mesh):
    placed = (
        P("ctx", "head"),
        P("ctx", "head"),
        P("head", None, None),
        P("head", None, None),
        P("head", None),
        P(None, "ctx"),
        P(),
    )
    return jax.shard_map(
        functools.partial(on_device, mesh.shape["ctx"], mesh.shape["head"]),
        mesh=mesh, in_specs=placed, out_specs=P("ctx", "head"), check_vma=False,
    )
```

time: 71.4 us -> 63.3 us (0.89)
  the two profiles are of different devices: /device:TPU:6 before, /device:TPU:0 now
where the time goes in v1:
time: 63.3 us; the launch traced here: 63.1 us
  Pallas kernels  60.8 us (96%)
  local copies, waits for them, and re-layouts  1.64 us (3%)
  between operations  0.66 us (1%)
    pallas_call x1, Pallas kernels, on_device(): pl.pallas_call(functools.partial(kernel, devices, heads_axis, tokens, hal...  60.8 us
    unnamed x1, local copies, waits for them, and re-layouts  1.64 us

profile of v1, /device:TPU:0, one launch (start us, length us, event | category | flops | bytes accessed | tf_op | source)
XLA Modules:
  0.0 63.1 jit_solution(5496203351468426714)
XLA Ops:
  0.7 60.8 %shard_map.73 = bf16[64,1792]{1,0:T(8,128)(2,1)} custom-call(s32[1]{0:T(128)S(6)} %copy.9.start_ref, bf16[64,2048]{1,0:T(8,128)(2,1)} %qn_hbm.1, bf16[64,1024]{1,0:T(8,128)(2,1)} %qr_hbm.1, bf16[16,128,512]{2,1,0:T(8,128)(2,1)} %uk_hbm.1, bf16[16,512,128]{2,1,0:T(8,128)(2,1)} %uv_hbm.1, bf16[2048,7168]{1,0:T(8,128)(2,1)} %wo_hbm.1, bf16[576,1024]{1,0:T(8,128)(2,1)} %cache_hbm.1), custom_call_target="tpu_custom_call" | custom-call | tf_op jit(solution)/shard_map/pallas_call | solution.py:426
  61.5 1.6 %copy.10 = bf16[64,1792]{1,0:T(8,128)(2,1)} copy(bf16[64,1792]{1,0:T(8,128)(2,1)} %shard_map.73) | data formatting | bytes 458752

commit v2 on v1

--- a/solution.py
+++ b/solution.py
@@ -191,6 +191,25 @@
             source_chip = peer_chip(chip, step, chips)
             for c in range(2):
                 sources.append(source_chip * 2 + c)
+        lanes = lax.broadcasted_iota(jnp.int32, (1, lanes_total), 1)
+        token = jnp.zeros((1, lanes_total), jnp.int32)
+        for i, src in enumerate(sources):
+            token = jnp.where(
+                lanes // part_rows == i,
+                src * tokens + phase * part_rows + lanes - i * part_rows, token,
+            )
+        position = token + group_start
+
+        def fill(i, carry):
+            here = pl.multiple_of(i * chunk, chunk)
+            slot = lax.broadcasted_iota(jnp.int32, (chunk, lanes_total), 0) + (chip * span + here)
+            bias[pl.ds(here, chunk), :] = jnp.where(slot <= position, 0.0, masked_score)
+            return carry
+
+        lax.fori_loop(0, span // chunk, fill, 0)
+
+        for step in order:
+            source_chip = peer_chip(chip, step, chips)
             if step == 0:
                 own_q[2 * phase].wait()
                 own_q[2 * phase + 1].wait()
@@ -201,22 +220,6 @@
                     src = source_chip * 2 + c
                     for copy in q_copies(phase, src, core, src, step * 2 + c, step * 2 + c):
                         copy.wait_recv()
-        lanes = lax.broadcasted_iota(jnp.int32, (1, lanes_total), 1)
-        token = jnp.zeros((1, lanes_total), jnp.int32)
-        for i, src in enumerate(sources):
-            token = jnp.where(
-                lanes // part_rows == i,
-                src * tokens + phase * part_rows + lanes - i * part_rows, token,
-            )
-        position = token + group_start
-
-        def fill(i, carry):
-            here = pl.multiple_of(i * chunk, chunk)
-            slot = lax.broadcasted_iota(jnp.int32, (chunk, lanes_total), 0) + (chip * span + here)
-            bias[pl.ds(here, chunk), :] = jnp.where(slot <= position, 0.0, masked_score)
-            return carry
-
-        lax.fori_loop(0, span // chunk, fill, 0)
 
         token_rows = slice(phase * part_rows, (phase + 1) * part_rows)
 
@@ -258,7 +261,7 @@
                     lse_send[phase, i, pl.ds(h, 1), :] = lse[:, 2 * i * pair:2 * (i + 1) * pair]
             return carry
 
-        lax.fori_loop(0, half // 2, head_pair, 0)
+        lax.fori_loop(0, half // 2, head_pair, 0, unroll=2)
 
         for i, step in enumerate(order):
             target_chip = peer_chip(chip, step, chips)

time: 63.3 us -> 60.7 us (0.959)
  Pallas kernels: 60.8 us -> 58.3 us
    pallas_call x1, Pallas kernels: 60.8 us -> 58.3 us  [on_device(): pl.pallas_call(functools.partial(kernel, devices, heads_axis, tokens, hal...]
where the time goes in v2:
time: 60.7 us; the launch traced here: 60.6 us
  Pallas kernels  58.3 us (96%)
  local copies, waits for them, and re-layouts  1.64 us (3%)
  between operations  0.66 us (1%)
    pallas_call x1, Pallas kernels, on_device(): pl.pallas_call(functools.partial(kernel, devices, heads_axis, tokens, hal...  58.3 us
    unnamed x1, local copies, waits for them, and re-layouts  1.64 us

profile of v2, /device:TPU:0, one launch (start us, length us, event | category | flops | bytes accessed | tf_op | source)
XLA Modules:
  0.0 60.6 jit_solution(8792599390800795724)
XLA Ops:
  0.7 58.3 %shard_map.73 = bf16[64,1792]{1,0:T(8,128)(2,1)} custom-call(s32[1]{0:T(128)S(6)} %copy.9.start_ref, bf16[64,2048]{1,0:T(8,128)(2,1)} %qn_hbm.1, bf16[64,1024]{1,0:T(8,128)(2,1)} %qr_hbm.1, bf16[16,128,512]{2,1,0:T(8,128)(2,1)} %uk_hbm.1, bf16[16,512,128]{2,1,0:T(8,128)(2,1)} %uv_hbm.1, bf16[2048,7168]{1,0:T(8,128)(2,1)} %wo_hbm.1, bf16[576,1024]{1,0:T(8,128)(2,1)} %cache_hbm.1), custom_call_target="tpu_custom_call" | custom-call | tf_op jit(solution)/shard_map/pallas_call | solution.py:429
  58.9 1.6 %copy.10 = bf16[64,1792]{1,0:T(8,128)(2,1)} copy(bf16[64,1792]{1,0:T(8,128)(2,1)} %shard_map.73) | data formatting | bytes 458752
